TPU v7x, 32 devices: a whole 2x2x4 slice. The times are simulated.
32 devices in a mesh: clip: 2 (over x), seq: 16 (over z, y, core).
Axes of the slice: x: 2, y: 2, z: 4, core: 2. Of those that a mesh axis runs over, the one named last changes fastest.
Arguments:
- hidden: bfloat16 [2, 1792, 1536], P(None, ('clip', 'seq')), parts along dimension 1, may hold values from -6 to 6
- latent: float32 [1792, 100], P(('clip', 'seq')), parts along dimension 0, may hold values from -6 to 6
- lengths: int32 [2], P('clip'), parts along dimension 0, may hold values from 448 to 896
- step_index: int32 [1], replicated, may hold values from 0 to 31
- guidance: float32 [1], replicated, may hold values from 1.5 to 2.5
- modulation: float32 [5, 1536], replicated, may hold values from -2.5 to 2.5
- conv_kernel: float32 [31, 1536], replicated, may hold values from -1 to 1
- w_qkv: bfloat16 [1536, 3072], replicated, may hold values from -1 to 1
- w_out: bfloat16 [1024, 1536], replicated, may hold values from -0.1875 to 0.1875
- w_mel: bfloat16 [1536, 100], replicated, may hold values from -0.15625 to 0.15625
Outputs:
- velocity: float32 [1792, 100], P(('clip', 'seq')), parts along dimension 0
- estimate: float32 [1792, 100], P(('clip', 'seq')), parts along dimension 0
There are 2 independent parts, one for each index of `clip`. A program takes and returns all parts, laid end to end along the dimension named above; an argument that names none is the same for every part. Nothing has to cross between parts.
All inputs are finite; a program needn't handle non-finite values.
Results may differ from a plain program's by a relative error of at most 0.0061.
Values may be sent and summed in bfloat16 or wider, within the bound.
No kernel may reach another device: no remote copies, remote signals or barrier semaphores. Data moves between devices by JAX's collectives and lax.ppermute only.
A program may use at most 192 MiB of HBM per device.

v0:
```python
import jax
import jax.numpy as jnp
from jax import lax
from jax.sharding import PartitionSpec as P

HEADS = 16
HEAD_DIM = 64
KERNEL = 31
STEPS = 32


EPSILON = 1e-06
NEGATIVE = -1e30


def extended(cells, sides, width):
    for axis, dim in sides:
        count = lax.axis_size(axis)
        ends = count - 1
        head = lax.slice_in_dim(cells, 0, width, axis=dim)
        tail = lax.slice_in_dim(cells, cells.shape[dim] - width, cells.shape[dim], axis=dim)
        cells = jnp.concatenate(
            [
                lax.ppermute(tail, axis, [(i, (i + 1) % count) for i in range(ends)]),
                cells,
                lax.ppermute(head, axis, [((i + 1) % count, i) for i in range(ends)]),
            ],
            axis=dim,
        )
    return cells


def from_partner(shard, axis, apart):
    return lax.ppermute(shard, axis, [(i, i ^ 1 << apart) for i in range(lax.axis_size(axis))])


def layer_norm(values, shift_row, scale_row):
    mean_value = jnp.mean(values, axis=-1, keepdims=True)
    centered = values - mean_value
    variance = jnp.mean(centered * centered, axis=-1, keepdims=True)
    return centered * lax.rsqrt(variance + EPSILON) * (1.0 + scale_row) + shift_row


def mish(values):
    return values * jnp.tanh(jax.nn.softplus(values))


def rotate(values, positions):
    half_dim = values.shape[-1] // 2
    inverse = 10000.0 ** (-jnp.arange(half_dim, dtype=jnp.float32) / half_dim)
    angles = positions.astype(jnp.float32)[:, None] * inverse[None, :]
    cosine = jnp.cos(angles)[:, None, :]
    sine_table = jnp.sin(angles)[:, None, :]
    lower_half = values[..., :half_dim]
    upper_half = values[..., half_dim:]
    return jnp.concatenate(
        [
            lower_half * cosine - upper_half * sine_table,
            upper_half * cosine + lower_half * sine_table,
        ],
        axis=-1,
    )


def to_groups(values, subs):
    copies, frame_rows, _ = values.shape
    grouped = values.reshape(copies, subs, frame_rows // subs, HEADS, HEAD_DIM).transpose(
        0, 3, 1, 2, 4
    )
    return grouped.reshape(copies * HEADS * subs, frame_rows // (2 * subs), 2 * HEAD_DIM)


def from_groups(grouped, copies, frame_rows, subs):
    split = grouped.reshape(copies, HEADS, subs, frame_rows // subs, HEAD_DIM).transpose(
        0, 2, 3, 1, 4
    )
    return split.reshape(copies, frame_rows, HEADS * HEAD_DIM)


def block_size_for(row_total):
    for candidate in range(1024, 7, -8):
        if row_total % candidate == 0:
            return candidate
    return row_total


def attend_local(query_flat, key_flat, value_flat, key_live):
    groups, query_total, _ = query_flat.shape
    block_rows = block_size_for(query_total)
    blocks = query_flat.reshape(groups, query_total // block_rows, block_rows, HEAD_DIM).transpose(
        1, 0, 2, 3
    )
    scale_factor = HEAD_DIM ** (-0.5)
    live_mask = key_live[None, None, :]

    def one_block(block):
        scores = (
            jnp.einsum("gqd,gkd->gqk", block, key_flat, preferred_element_type=jnp.float32)
            * scale_factor
        )
        scores = jnp.where(live_mask, scores, NEGATIVE)
        row_peak = jnp.max(scores, axis=-1, keepdims=True)
        weights = jnp.where(live_mask, jnp.exp(scores - row_peak), 0.0)
        weight_sum = jnp.sum(weights, axis=-1)
        weighted = jnp.einsum(
            "gqk,gkd->gqd",
            weights.astype(jnp.bfloat16),
            value_flat,
            preferred_element_type=jnp.float32,
        )
        return (weighted / weight_sum[..., None]).astype(jnp.bfloat16)

    results = lax.map(one_block, blocks)
    return results.transpose(1, 0, 2, 3).reshape(groups, query_total, HEAD_DIM)


def per_device(
    hidden, latent, lengths, step_index, guidance, modulation, conv_kernel, w_qkv, w_out, w_mel
):
    copies, frame_rows, model_width = hidden.shape
    offset = lax.axis_index("seq") * frame_rows
    positions = offset + jnp.arange(frame_rows, dtype=jnp.int32)
    length = lengths[0]
    is_live = positions < length
    masked = hidden * is_live[None, :, None].astype(jnp.bfloat16)
    half_width = KERNEL // 2
    padded = extended(masked, (("seq", 1),), half_width)
    convolved = jnp.zeros(hidden.shape, jnp.float32)
    for tap_index in range(KERNEL):
        convolved = convolved + conv_kernel[tap_index] * padded[
            :, tap_index : tap_index + frame_rows, :
        ].astype(jnp.float32)
    residual = hidden.astype(jnp.float32) + mish(convolved)
    normed = layer_norm(residual, modulation[0], modulation[1]).astype(jnp.bfloat16)
    projected = jnp.dot(normed.reshape(-1, model_width), w_qkv, preferred_element_type=jnp.float32)
    projected = projected.reshape(copies, frame_rows, 3, HEADS, HEAD_DIM)
    queries = rotate(projected[:, :, 0], positions).astype(jnp.bfloat16)
    keys_all = (
        rotate(projected[:, :, 1], positions)
        .astype(jnp.bfloat16)
        .reshape(copies, frame_rows, HEADS * HEAD_DIM)
    )
    values_all = (
        projected[:, :, 2].astype(jnp.bfloat16).reshape(copies, frame_rows, HEADS * HEAD_DIM)
    )
    seq_size = lax.axis_size("seq")
    subs = max(1, seq_size // (2 * HEADS))
    sub_index = lax.axis_index("seq") % subs
    part_rows = frame_rows // subs
    queries_flat = queries.reshape(copies, frame_rows, HEADS * HEAD_DIM)
    sent = (to_groups(queries_flat, subs), to_groups(keys_all, subs), to_groups(values_all, subs))
    query_group, key_group, value_group = (
        lax.all_to_all(sent[0], "seq", split_axis=0, concat_axis=1, tiled=True),
        lax.all_to_all(sent[1], "seq", split_axis=0, concat_axis=1, tiled=True),
        lax.all_to_all(sent[2], "seq", split_axis=0, concat_axis=1, tiled=True),
    )

    def key_positions(sub_id):
        source_start = jnp.arange(seq_size, dtype=jnp.int32)[:, None] * frame_rows
        return (
            source_start + sub_id * part_rows + jnp.arange(part_rows, dtype=jnp.int32)[None, :]
        ).reshape(-1)

    key_rows = key_positions(sub_index)
    if subs > 1:
        other_keys, other_values = from_partner((key_group, value_group), "seq", 0)
        key_group = jnp.concatenate([key_group, other_keys], axis=1)
        value_group = jnp.concatenate([value_group, other_values], axis=1)
        key_rows = jnp.concatenate([key_rows, key_positions(1 - sub_index)])
    groups = query_group.shape[0]
    query_flat = query_group.reshape(groups, -1, HEAD_DIM)
    key_flat = key_group.reshape(groups, -1, HEAD_DIM)
    value_flat = value_group.reshape(groups, -1, HEAD_DIM)
    attended_group = attend_local(query_flat, key_flat, value_flat, key_rows < length)
    returned = lax.all_to_all(
        attended_group.reshape(groups, -1, 2 * HEAD_DIM),
        "seq",
        split_axis=1,
        concat_axis=0,
        tiled=True,
    )
    attended = from_groups(returned, copies, frame_rows, subs)
    branch = jnp.dot(
        attended.reshape(copies * frame_rows, -1), w_out, preferred_element_type=jnp.float32
    )
    after = residual + modulation[2] * branch.reshape(copies, frame_rows, model_width)
    final_norm = layer_norm(after, modulation[3], modulation[4]).astype(jnp.bfloat16)
    speed = jnp.dot(final_norm.reshape(-1, model_width), w_mel, preferred_element_type=jnp.float32)
    speed = speed.reshape(copies, frame_rows, -1)
    guided = speed[0] + guidance[0] * (speed[0] - speed[1])
    velocity = jnp.where(is_live[:, None], guided, 0.0)
    progress = step_index[0].astype(jnp.float32) / STEPS
    time_now = 1.0 - jnp.cos(0.5 * jnp.pi * progress)
    estimate = latent + (1.0 - time_now) * velocity
    return (velocity, estimate)


def solution(mesh):
    return jax.shard_map(
        per_device,
        mesh=mesh,
        in_specs=(
            P(None, ("clip", "seq"), None),
            P(("clip", "seq"), None),
            P("clip"),
            P(),
            P(),
            P(),
            P(),
            P(),
            P(),
            P(),
        ),
        out_specs=(P(("clip", "seq"), None), P(("clip", "seq"), None)),
        check_vma=False,
    )
```

profile of v0, /device:TPU:0, one launch (start us, length us, event | category | flops | bytes accessed | tf_op | source)
XLA Modules:
  0.0 131.8 jit_solution(2257580926688157541)
XLA Ops:
  1.5 1.2 broadcast_multiply_fusion
  2.7 0.7 fusion.78
  3.4 3.0 %collective-permute-start = (bf16[2,15,1536]{2,1,0:T(8,128)(2,1)}, bf16[2,15,1536]{2,1,0:T(8,128)(2,1)}, u32[]{:S(2)}, u32[]{:S(2)}) collective-permute-start(bf16[2,15,1536]{2,1,0:T(8,128)(2,1)} %get-tuple-element.74), channel_id=1, source_target_pairs={{0,1},{1,2},{2,3},{3,4},{4,5},{5,6},{6,7},{7,8},{8,9},{9,10},{10,1... | collective-permute-start | bytes 276488 | tf_op jit(solution)/shard_map/ppermute | solution.py:24
  6.4 1.3 collective-permute-start.1
  7.7 2.5 %slice_reduce_fusion.33 = (f32[1536]{0:T(1024)S(1)}, f32[1536]{0:T(1024)S(1)}, f32[1536]{0:T(1024)S(1)}, f32[1536]{0:T(1024)S(1)}, f32[1536]{0:T(1024)S(1)}, /*i...) fusion(f32[31,1536]{1,0:T(8,128)} %param.16), kind=kLoop, calls=%fused_computation.177 | loop fusion | bytes 233472 | tf_op jit(solution)/shard_map/slice | solution.py:130
  10.2 2.1 %slice_reduce_fusion.32 = (f32[1536]{0:T(1024)}, f32[1536]{0:T(1024)}, f32[1536]{0:T(1024)}, f32[1536]{0:T(1024)}, f32[1536]{0:T(1024)}, /*index=5*/f32[1536]{0:...) fusion(f32[31,1536]{1,0:T(8,128)} %param.16), kind=kLoop, calls=%fused_computation.176 | loop fusion | bytes 147456 | tf_op jit(solution)/shard_map/slice | solution.py:130
  12.3 12.7 %copy.34 = bf16[1536,3072]{0,1:T(8,128)(2,1)} copy(bf16[1536,3072]{1,0:T(8,128)(2,1)} %param.17) | data formatting | bytes 18874368 | tf_op args[7]
  25.2 1.7 %add_reduce_fusion = (f32[1536]{0:T(1024)S(1)}, f32[1536]{0:T(1024)S(1)}, f32[1536]{0:T(1024)S(1)}, f32[1536]{0:T(1024)}, f32[1536]{0:T(1024)}) fusion(f32[5,1536]{1,0:T(8,128)} %param.15), kind=kLoop, calls=%fused_computation.143 | loop fusion | flops 3072 | bytes 61440 | tf_op jit(solution)/shard_map/add | solution.py:41
  26.9 8.2 %fusion.74 = (f32[2,56]{1,0:T(2,128)S(1)}, f32[2,56,1536]{2,1,0:T(8,128)S(1)}) fusion(bf16[2,15,1536]{2,1,0:T(8,128)(2,1)} %collective-permute-done.1, bf16[2,56,1536]{2,1,0:T(8,128)(2,1)S(1)} %broadcast_multiply_fusion, f32[1536]{0:T(1024)} %get-tuple-element.55, f32[1536]{0:T(1024)} %get-tuple-element.56, f32[1536]{0:T(1024)S(1)} %get-tuple-element.27, ...), kind=kLoop, calls=%fused_computation.189 | loop fusion | flops 33030032 | bytes 1751488 | tf_op jit(solution)/shard_map/reduce_sum | solution.py:38
  35.2 0.2 multiply_reduce_fusion.1
  35.4 7.3 %fusion.60 = f32[2,56,3,16,64]{4,1,3,2,0:T(8,128)S(1)} fusion(bf16[3,16,64,1536,1]{3,2,1,0,4:T(8,128)(2,1)} %bitcast.90, f32[2,56,1536]{2,1,0:T(8,128)S(1)} %get-tuple-element.65, f32[1536]{0:T(1024)S(1)} %get-tuple-element.58, f32[1536]{0:T(1024)S(1)} %get-tuple-element.59, f32[2,56]{1,0:T(2,128)S(1)} %add_rsqrt_fusion.1, ...), kind=kOutput, calls=%fused_computation.123 | convolution fusion | flops 1057824768 | bytes 11514752 | tf_op jit(solution)/shard_map/dot_general | solution.py:135
  42.9 1.7 %fusion.28 = (bf16[2,1,56,16,32]{4,2,3,0,1:T(8,128)(2,1)S(1)}, bf16[2,1,56,16,32]{4,2,3,0,1:T(8,128)(2,1)S(1)}, bf16[2,1,56,16,32]{4,2,3,0,1:T(8,128)(2,1)}, bf16[2,1,56,16,32]{4,2,3,0,1:T(8,128)(2,1)}) fusion(f32[2,56,16,64]{3,1,2,0:T(8,128)S(1)} %get-tuple-element.68, f32[56,32]{1,0:T(8,128)S(1)} %get-tuple-element.79, f32[56,32]{1,0:T(8,128)S(1)} %get-tuple-element.78, ...), kind=kLoop, calls=%fused_computation.61 | loop fusion | flops 917504 | bytes 1390592 | tf_op jit(solution)/shard_map/concatenate | solution.py:56
  44.5 1.0 maximum_bitcast_fusion.1
  45.6 2.0 %reshape.294 = bf16[32,28,128]{2,1,0:T(8,128)(2,1)} reshape(bf16[2,16,1,56,64]{4,3,1,0,2:T(8,128)(2,1)} %maximum_bitcast_fusion.1) | data formatting | bytes 458752 | tf_op jit(solution)/shard_map/reshape | solution.py:70
  47.5 8.7 %all-to-all-start.1 = ((bf16[32,28,128]{2,1,0:T(8,128)(2,1)}), bf16[32,28,128]{2,1,0:T(8,128)(2,1)S(1)}, u32[]{:S(2)}, u32[]{:S(2)}) async-start(bf16[32,28,128]{2,1,0:T(8,128)(2,1)} %reshape.294), calls=%async_computation.1 | async-start | bytes 524288 | tf_op jit(solution)/shard_map/all_to_all | solution.py:154
  56.2 2.2 %maximum_bitcast_fusion = bf16[2,16,1,56,64]{4,3,1,0,2:T(8,128)(2,1)} fusion(bf16[2,1,56,16,32]{4,2,3,0,1:T(8,128)(2,1)} %get-tuple-element.76, bf16[2,1,56,16,32]{4,2,3,0,1:T(8,128)(2,1)} %get-tuple-element.77), kind=kLoop, calls=%fused_computation.64 | loop fusion | flops 458752 | bytes 458752 | tf_op jit(solution)/shard_map/transpose | solution.py:67
  58.4 2.0 %reshape.293 = bf16[32,28,128]{2,1,0:T(8,128)(2,1)} reshape(bf16[2,16,1,56,64]{4,3,1,0,2:T(8,128)(2,1)} %maximum_bitcast_fusion) | data formatting | bytes 458752 | tf_op jit(solution)/shard_map/reshape | solution.py:70
  60.4 5.9 %all-to-all-done.1 = bf16[32,28,128]{2,1,0:T(8,128)(2,1)S(1)} async-done(((bf16[32,28,128]{2,1,0:T(8,128)(2,1)}), bf16[32,28,128]{2,1,0:T(8,128)(2,1)S(1)}, u32[]{:S(2)}, u32[]{:S(2)}) %all-to-all-start.1) | async-done | bytes 229408 | tf_op jit(solution)/shard_map/all_to_all | solution.py:154
  66.2 4.2 %all-to-all-start = ((bf16[32,28,128]{2,1,0:T(8,128)(2,1)}), bf16[32,28,128]{2,1,0:T(8,128)(2,1)}, u32[]{:S(2)}, u32[]{:S(2)}) async-start(bf16[32,28,128]{2,1,0:T(8,128)(2,1)} %reshape.293), calls=%async_computation | async-start | bytes 524288 | tf_op jit(solution)/shard_map/all_to_all | solution.py:153
  70.4 2.0 %fusion.30 = bf16[2,16,1,56,64]{4,3,1,0,2:T(8,128)(2,1)} fusion(f32[2,56,3,16,64]{4,1,3,2,0:T(8,128)} %copy-done.2), kind=kLoop, calls=%fused_computation.63 | loop fusion | bytes 458752 | tf_op jit(solution)/shard_map/transpose | solution.py:67
  72.5 2.0 %reshape.296 = bf16[32,28,128]{2,1,0:T(8,128)(2,1)} reshape(bf16[2,16,1,56,64]{4,3,1,0,2:T(8,128)(2,1)} %fusion.30) | data formatting | bytes 458752 | tf_op jit(solution)/shard_map/reshape | solution.py:70
  74.4 6.0 %all-to-all-done = bf16[32,28,128]{2,1,0:T(8,128)(2,1)} async-done(((bf16[32,28,128]{2,1,0:T(8,128)(2,1)}), bf16[32,28,128]{2,1,0:T(8,128)(2,1)}, u32[]{:S(2)}, u32[]{:S(2)}) %all-to-all-start) | async-done | bytes 229408 | tf_op jit(solution)/shard_map/all_to_all | solution.py:153
  80.4 4.4 %all-to-all-start.2 = ((bf16[32,28,128]{2,1,0:T(8,128)(2,1)}), bf16[32,28,128]{2,1,0:T(8,128)(2,1)}, u32[]{:S(2)}, u32[]{:S(2)}) async-start(bf16[32,28,128]{2,1,0:T(8,128)(2,1)} %reshape.296), calls=%async_computation.2 | async-start | bytes 524288 | tf_op jit(solution)/shard_map/all_to_all | solution.py:155
  85.0 0.7 copy.60
  85.7 2.0 %reshape.295 = bf16[2,896,64]{2,1,0:T(8,128)(2,1)} reshape(bf16[2,16,28,128]{3,2,1,0:T(8,128)(2,1)} %bitcast.94) | data formatting | bytes 458752 | tf_op jit(solution)/shard_map/reshape | solution.py:172
  87.7 1.0 copy.61
  88.7 1.0 squeeze.26
  89.7 4.9 %all-to-all-done.2 = bf16[32,28,128]{2,1,0:T(8,128)(2,1)} async-done(((bf16[32,28,128]{2,1,0:T(8,128)(2,1)}), bf16[32,28,128]{2,1,0:T(8,128)(2,1)}, u32[]{:S(2)}, u32[]{:S(2)}) %all-to-all-start.2) | async-done | bytes 229408 | tf_op jit(solution)/shard_map/all_to_all | solution.py:155
  94.7 1.0 copy.59
  95.6 1.0 reshape.297
  96.6 5.7 %fusion.79 = (f32[2,896]{1,0:T(2,128)S(1)}, bf16[2,896,896]{1,2,0:T(8,128)(2,1)}) fusion(pred[896]{0:T(1024)(128)(4,1)S(1)} %lt.36, bf16[2,896,64]{2,1,0:T(8,128)(2,1)} %squeeze.26, bf16[2,896,64]{2,1,0:T(8,128)(2,1)} %reshape.295), kind=kOutput, calls=%fused_computation.192 | convolution fusion | flops 215155584 | bytes 3678080 | tf_op jit(solution)/shard_map/while/body/eval_jaxpr/sub | solution.py:103
  102.4 2.7 %fusion.18 = bf16[2,896,64]{1,2,0:T(8,128)(2,1)S(1)} fusion(bf16[2,896,64]{2,1,0:T(8,128)(2,1)} %reshape.297, bf16[2,896,896]{1,2,0:T(8,128)(2,1)} %get-tuple-element.81, f32[2,896]{1,0:T(2,128)S(1)} %get-tuple-element.80), kind=kOutput, calls=%fused_computation.43 | convolution fusion | flops 205750272 | bytes 3677184 | tf_op jit(solution)/shard_map/while/body/eval_jaxpr/gqk,gkd->gqd/dot_general | solution.py:105
  105.0 1.0 copy.43
  106.0 1.3 reshape_reshape_transpose.3
  107.3 0.9 copy.44
  108.2 3.5 %all-to-all-start.3 = ((bf16[2,448,128]{2,0,1:T(2,128)(2,1)}), bf16[2,448,128]{2,0,1:T(2,128)(2,1)S(1)}, u32[]{:S(2)}, u32[]{:S(2)}) async-start(bf16[2,448,128]{2,0,1:T(2,128)(2,1)} %copy.44), calls=%async_computation.3 | async-start | bytes 458752 | tf_op jit(solution)/shard_map/all_to_all | solution.py:175
  113.2 8.0 %all-to-all-done.3 = bf16[2,448,128]{2,0,1:T(2,128)(2,1)S(1)} async-done(((bf16[2,448,128]{2,0,1:T(2,128)(2,1)}), bf16[2,448,128]{2,0,1:T(2,128)(2,1)S(1)}, u32[]{:S(2)}, u32[]{:S(2)}) %all-to-all-start.3) | async-done | bytes 229408 | tf_op jit(solution)/shard_map/all_to_all | solution.py:175
  121.2 0.7 copy-done.3
  121.9 1.0 copy.45
  122.8 1.0 reshape.298
  123.9 1.9 %copy.46 = bf16[2,1,56,16,64]{4,3,2,0,1:T(8,128)(2,1)} copy(bf16[2,1,56,16,64]{4,2,3,0,1:T(8,128)(2,1)} %bitcast.91) | data formatting | bytes 458752 | tf_op jit(solution)/shard_map/transpose | solution.py:74
  125.7 1.4 %dot_general.28 = bf16[2,56,1024]{2,1,0:T(8,128)(2,1)S(1)} reshape(bf16[2,1,56,16,64]{4,3,2,0,1:T(8,128)(2,1)} %copy.46) | data formatting | bytes 458752 | tf_op jit(solution)/shard_map/dot_general | solution.py:183
  127.1 1.8 %fusion.80 = (f32[2,56]{1,0:T(2,128)S(1)}, f32[2,56,1536]{2,1,0:T(8,128)S(1)}) fusion(f32[2,56,1536]{2,1,0:T(8,128)} %copy-done.1, bf16[2,56,1024]{2,1,0:T(8,128)(2,1)S(1)} %dot_general.28, bf16[1024,1536]{1,0:T(8,128)(2,1)S(1)} %copy-done, f32[1536]{0:T(1024)S(1)} %copy-done.5), kind=kOutput, calls=%fused_computation.193 | convolution fusion | flops 352837504 | bytes 4757952 | tf_op jit(solution)/shard_map/dot_general | solution.py:183
  129.0 0.2 multiply_reduce_fusion
  129.2 0.9 add_convert_fusion.2
  130.1 0.2 fusion.81
  130.5 0.7 copy.48
  131.1 0.7 copy.49
  (29 shorter events, 0.8 us)
Async XLA Ops:
  0.6 126.5 %copy-start = (bf16[1024,1536]{1,0:T(8,128)(2,1)S(1)}, bf16[1024,1536]{1,0:T(8,128)(2,1)}, u32[]{:S(2)}) copy-start(bf16[1024,1536]{1,0:T(8,128)(2,1)} %param.18) | copy-start | bytes 9437188
  3.4 23.6 %collective-permute-start = (bf16[2,15,1536]{2,1,0:T(8,128)(2,1)}, bf16[2,15,1536]{2,1,0:T(8,128)(2,1)}, u32[]{:S(2)}, u32[]{:S(2)}) collective-permute-start(bf16[2,15,1536]{2,1,0:T(8,128)(2,1)} %get-tuple-element.74), channel_id=1, source_target_pairs={{0,1},{1,2},{2,3},{3,4},{4,5},{5,6},{6,7},{7,8},{8,9},{9,10},{10,1... | collective-permute-start | bytes 276488 | tf_op jit(solution)/shard_map/ppermute | solution.py:24
  6.4 20.5 %collective-permute-start.1 = (bf16[2,15,1536]{2,1,0:T(8,128)(2,1)}, bf16[2,15,1536]{2,1,0:T(8,128)(2,1)}, u32[]{:S(2)}, u32[]{:S(2)}) collective-permute-start(bf16[2,15,1536]{2,1,0:T(8,128)(2,1)} %get-tuple-element.75), channel_id=1, source_target_pairs={{1,0},{2,1},{3,2},{4,3},{5,4},{6,5},{7,6},{8,7},{9,8},{10,9},{11,1... | collective-permute-start | bytes 276488 | tf_op jit(solution)/shard_map/ppermute | solution.py:26
  35.2 7.5 %copy-start.1 = (f32[2,56,1536]{2,1,0:T(8,128)}, f32[2,56,1536]{2,1,0:T(8,128)S(1)}, u32[]{:S(2)}) copy-start(f32[2,56,1536]{2,1,0:T(8,128)S(1)} %get-tuple-element.65) | copy-start | bytes 2064388
  42.7 1.8 %copy-start.2 = (f32[2,56,3,16,64]{4,1,3,2,0:T(8,128)}, f32[2,56,3,16,64]{4,1,3,2,0:T(8,128)S(1)}, u32[]{:S(2)}) copy-start(f32[2,56,3,16,64]{4,1,3,2,0:T(8,128)S(1)} %fusion.60) | copy-start | bytes 4128772
  47.5 18.7 %all-to-all-start.1 = ((bf16[32,28,128]{2,1,0:T(8,128)(2,1)}), bf16[32,28,128]{2,1,0:T(8,128)(2,1)S(1)}, u32[]{:S(2)}, u32[]{:S(2)}) async-start(bf16[32,28,128]{2,1,0:T(8,128)(2,1)} %reshape.294), calls=%async_computation.1 | async-start | bytes 524288 | tf_op jit(solution)/shard_map/all_to_all | solution.py:154
  66.2 14.2 %all-to-all-start = ((bf16[32,28,128]{2,1,0:T(8,128)(2,1)}), bf16[32,28,128]{2,1,0:T(8,128)(2,1)}, u32[]{:S(2)}, u32[]{:S(2)}) async-start(bf16[32,28,128]{2,1,0:T(8,128)(2,1)} %reshape.293), calls=%async_computation | async-start | bytes 524288 | tf_op jit(solution)/shard_map/all_to_all | solution.py:153
  80.4 14.2 %all-to-all-start.2 = ((bf16[32,28,128]{2,1,0:T(8,128)(2,1)}), bf16[32,28,128]{2,1,0:T(8,128)(2,1)}, u32[]{:S(2)}, u32[]{:S(2)}) async-start(bf16[32,28,128]{2,1,0:T(8,128)(2,1)} %reshape.296), calls=%async_computation.2 | async-start | bytes 524288 | tf_op jit(solution)/shard_map/all_to_all | solution.py:155
  102.4 9.4 %copy-start.6 = (f32[56,100]{1,0:T(8,128)S(1)}, f32[56,100]{1,0:T(8,128)}, u32[]{:S(2)}) copy-start(f32[56,100]{1,0:T(8,128)} %param.11) | copy-start | bytes 67204
  102.4 24.8 %copy-start.5 = (f32[1536]{0:T(1024)S(1)}, f32[1536]{0:T(1024)}, u32[]{:S(2)}) copy-start(f32[1536]{0:T(1024)} %get-tuple-element.60) | copy-start | bytes 18436
  108.2 13.0 %all-to-all-start.3 = ((bf16[2,448,128]{2,0,1:T(2,128)(2,1)}), bf16[2,448,128]{2,0,1:T(2,128)(2,1)S(1)}, u32[]{:S(2)}, u32[]{:S(2)}) async-start(bf16[2,448,128]{2,0,1:T(2,128)(2,1)} %copy.44), calls=%async_computation.3 | async-start | bytes 458752 | tf_op jit(solution)/shard_map/all_to_all | solution.py:175
  121.2 0.7 copy-start.3
  127.1 3.0 %copy-start.4 = (bf16[1536,100]{0,1:T(8,128)(2,1)S(1)}, bf16[1536,100]{0,1:T(8,128)(2,1)}, u32[]{:S(2)}) copy-start(bf16[1536,100]{0,1:T(8,128)(2,1)} %param.19) | copy-start | bytes 921604
where the time goes:
time: 134 us; the launch traced here: 132 us
  local copies, waits for them, and re-layouts  43.5 us (32%)
  starting transfers between devices  25.1 us (19%)
  waiting for transfers between devices  24.8 us (19%)
  other arithmetic  17.8 us (13%)
  matrix products  17.7 us (13%)
  between operations  3.05 us (2%)
    unnamed x18, local copies, waits for them, and re-layouts  14.9 us
    all_to_all x1, starting transfers between devices, per_device(): lax.all_to_all(sent[1], 'seq', split_axis=0, concat_axis=1, tiled=True)  8.67 us
    reduce_sum x1, other arithmetic, layer_norm(): mean_value = jnp.mean(values, axis=-1, keepdims=True)  8.24 us
    all_to_all x1, waiting for transfers between devices, per_device(): lax.all_to_all(attended_group.reshape(groups, -1, 2 * HEAD_DIM), 'seq', s...  7.96 us
    dot_general x1, matrix products, per_device(): jnp.dot(normed.reshape(-1, model_width), w_qkv, preferred_element_type=jn...  7.27 us
    all_to_all x1, waiting for transfers between devices, per_device(): lax.all_to_all(sent[0], 'seq', split_axis=0, concat_axis=1, tiled=True)  6.01 us
    reshape x3, local copies, waits for them, and re-layouts, to_groups(): grouped.reshape(copies * HEADS * subs, frame_rows // (2 * subs), 2 * HEAD...  5.91 us
    all_to_all x1, waiting for transfers between devices, per_device(): lax.all_to_all(sent[1], 'seq', split_axis=0, concat_axis=1, tiled=True)  5.86 us
  transfers between devices with their start and end apart: 6, of which 4 were waited for; matrix products, arithmetic and copies ran while one was open for 25% of the time, Pallas kernels for 0%

commit v1 on v0

v1 whole, which is shorter than its diff:
```python
import functools

import jax
import jax.numpy as jnp
from jax import lax
from jax.experimental import pallas as pl
from jax.experimental.pallas import tpu as pltpu
from jax.sharding import PartitionSpec as P

HEADS = 16
HEAD_DIM = 64
KERNEL = 31
STEPS = 32
LANES = 128


EPSILON = 1e-06
NEGATIVE = -1e30
VMEM = pltpu.VMEM
SMEM = pltpu.SMEM


def vmem_spec():
    return pl.BlockSpec(memory_space=VMEM)


def smem_spec():
    return pl.BlockSpec(memory_space=SMEM)


def hbm_spec():
    return pl.BlockSpec(memory_space=pl.ANY)


def rotary_tables(positions):
    half_dim = HEAD_DIM // 2
    inverse = 10000.0 ** (-jnp.arange(half_dim, dtype=jnp.float32) / half_dim)
    angles = positions.astype(jnp.float32)[:, None] * inverse[None, :]
    cosine = jnp.cos(angles)
    sine = jnp.sin(angles)
    return (
        jnp.concatenate([cosine, cosine, cosine, cosine], axis=1),
        jnp.concatenate([-sine, sine, -sine, sine], axis=1),
    )


def row_norm(load, store, tiles, width, mod_ref, row, total, rows_shape):
    mean = jnp.sum(total, axis=-1, keepdims=True) * (1.0 / width)

    def square(tile, acc):
        centered = load(tile) - mean
        return acc + centered * centered

    squares = lax.fori_loop(0, tiles, square, jnp.zeros(rows_shape, jnp.float32), unroll=2)
    variance = jnp.sum(squares, axis=-1, keepdims=True) * (1.0 / width)
    factor = lax.rsqrt(variance + EPSILON)

    def write(tile, carry):
        lanes = pl.ds(pl.multiple_of(tile * LANES, LANES), LANES)
        scale = 1.0 + mod_ref[row + 1 : row + 2, lanes]
        shift = mod_ref[row : row + 1, lanes]
        store(lanes, (load(tile) - mean) * factor * scale + shift)
        return carry

    lax.fori_loop(0, tiles, write, 0, unroll=2)


def front_kernel(
    info_ref, hidden_ref, left_ref, right_ref, taps_ref, mod_ref, cos_ref, sin_ref, weight_hbm,
    residual_ref, sent_ref, padded, normed, weight, sems,
):
    copies, rows, width = hidden_ref.shape
    halo = left_ref.shape[1]
    tiles = width // LANES
    depth = width // 8
    loads = [
        pltpu.make_async_copy(
            weight_hbm.at[pl.ds(i * depth, depth)], weight.at[pl.ds(i * depth, depth)], sems.at[i]
        )
        for i in range(8)
    ]
    for load in loads:
        load.start()
    length = info_ref[0]
    offset = info_ref[1]
    span = rows + 2 * halo
    frame = offset - halo + lax.broadcasted_iota(jnp.int32, (1, span, LANES), 1)
    live = (frame < length).astype(jnp.float32)
    first = halo - KERNEL // 2

    def convolve(tile, total):
        lanes = pl.ds(pl.multiple_of(tile * LANES, LANES), LANES)
        own = hidden_ref[:, :, lanes].astype(jnp.float32)
        padded[:, 0:halo] = left_ref[:, :, lanes].astype(jnp.float32) * live[:, 0:halo]
        padded[:, halo : halo + rows] = own * live[:, halo : halo + rows]
        padded[:, halo + rows : span] = (
            right_ref[:, :, lanes].astype(jnp.float32) * live[:, halo + rows : span]
        )
        acc = jnp.zeros((copies, rows, LANES), jnp.float32)
        for tap in range(KERNEL):
            acc = acc + taps_ref[tap : tap + 1, lanes][None] * padded[
                :, first + tap : first + tap + rows, :
            ]
        grown = jnp.exp(jnp.minimum(acc, 20.0))
        product = grown * (grown + 2.0)
        value = own + acc * (product / (product + 2.0))
        residual_ref[:, :, lanes] = value
        return total + value

    total = lax.fori_loop(0, tiles, convolve, jnp.zeros((copies, rows, LANES), jnp.float32))

    def load_tile(tile):
        return residual_ref[:, :, pl.ds(pl.multiple_of(tile * LANES, LANES), LANES)]

    def store_tile(lanes, value):
        normed[:, lanes] = value.reshape(copies * rows, LANES).astype(jnp.bfloat16)

    row_norm(
        load_tile, store_tile, tiles, width, mod_ref, 0, total,
        (copies, rows, LANES),
    )
    for load in loads:
        load.wait()
    blocks = sent_ref.shape[0] // copies
    wide = 2 * LANES
    cosine = jnp.concatenate([cos_ref[...]] * copies, axis=0)
    sine = jnp.concatenate([sin_ref[...]] * copies, axis=0)
    lane = lax.broadcasted_iota(jnp.int32, (copies * rows, LANES), 1)
    lower = lane % HEAD_DIM < HEAD_DIM // 2
    half = HEAD_DIM // 2
    for part in range(3):

        def project(block, carry):
            lanes = pl.ds(pl.multiple_of((part * blocks // 2 + block) * wide, wide), wide)
            both = jnp.dot(normed[...], weight[:, lanes], preferred_element_type=jnp.float32)
            for side in range(2):
                value = both[:, side * LANES : (side + 1) * LANES]
                if part < 2:
                    swapped = jnp.where(
                        lower, pltpu.roll(value, LANES - half, 1), pltpu.roll(value, half, 1)
                    )
                    value = value * cosine + swapped * sine
                value = value.astype(jnp.bfloat16)
                if part == 0:
                    value = value * jnp.bfloat16(HEAD_DIM**-0.5)
                value = value.astype(jnp.float32).reshape(copies, rows, LANES)
                for copy in range(copies):
                    sent_ref[copy * blocks + 2 * block + side, part] = value[copy].astype(
                        jnp.bfloat16
                    )
            return carry

        lax.fori_loop(0, blocks // 2, project, 0)


def attend_kernel(info_ref, got_ref, out_ref, keys, values_t, queries):
    groups, _, rows, _ = got_ref.shape
    key_total = groups * rows
    step = queries.shape[0] // 4
    length = info_ref[0]
    lane_low = lax.broadcasted_iota(jnp.int32, (rows, LANES), 1) < HEAD_DIM
    keys[...] = got_ref[:, 1].astype(jnp.float32).reshape(key_total, LANES).astype(jnp.bfloat16)
    values = got_ref[:, 2].astype(jnp.float32).reshape(key_total, LANES)
    values_t[...] = values.T.astype(jnp.bfloat16)
    queries[...] = jnp.zeros(queries.shape, jnp.bfloat16)
    live = lax.broadcasted_iota(jnp.int32, (key_total, 4 * step), 0) < length

    def one_pair(pair, carry):
        for at in range(2):
            query = got_ref[2 * pair + at, 0].astype(jnp.float32)
            queries[(2 * at) * step : (2 * at) * step + rows, :] = jnp.where(
                lane_low, query, 0.0
            ).astype(jnp.bfloat16)
            queries[(2 * at + 1) * step : (2 * at + 1) * step + rows, :] = jnp.where(
                lane_low, 0.0, query
            ).astype(jnp.bfloat16)
        scores = lax.dot_general(
            keys[...], queries[...], (((1,), (1,)), ((), ())), preferred_element_type=jnp.float32
        )
        scores = jnp.where(live, scores, NEGATIVE)
        peak = jnp.max(scores, axis=0, keepdims=True)
        weights = jnp.exp(scores - peak)
        weight_sum = jnp.sum(weights, axis=0, keepdims=True)
        mixed = jnp.dot(
            values_t[...], weights.astype(jnp.bfloat16), preferred_element_type=jnp.float32
        )
        mixed = (mixed / weight_sum).T
        for at in range(2):
            base = 2 * at * step
            out_ref[2 * pair + at] = jnp.where(
                lane_low, mixed[base : base + rows], mixed[base + step : base + step + rows]
            ).astype(jnp.bfloat16)
        return carry

    lax.fori_loop(0, groups // 2, one_pair, 0)


def back_kernel(
    info_ref, real_ref, got_ref, residual_ref, mod_ref, latent_ref, w_out_ref, w_mel_ref,
    velocity_ref, estimate_ref, attended, after,
):
    copies, rows, width = residual_ref.shape
    blocks = got_ref.shape[0] // copies
    tiles = width // LANES
    for block in range(blocks):
        pieces = [got_ref[copy * blocks + block].astype(jnp.float32) for copy in range(copies)]
        attended[:, block * LANES : (block + 1) * LANES] = jnp.concatenate(pieces, axis=0).astype(
            jnp.bfloat16
        )
    wide = 2 * LANES

    def project(block, total):
        lanes = pl.ds(pl.multiple_of(block * wide, wide), wide)
        branch = jnp.dot(attended[...], w_out_ref[:, lanes], preferred_element_type=jnp.float32)
        value = residual_ref[:, :, lanes].reshape(copies * rows, wide) + mod_ref[2:3, lanes] * branch
        after[:, lanes] = value
        return total + value[:, :LANES] + value[:, LANES:]

    total = lax.fori_loop(
        0, width // wide, project, jnp.zeros((copies * rows, LANES), jnp.float32)
    )
    final = after

    def load_tile(tile):
        return after[:, pl.ds(pl.multiple_of(tile * LANES, LANES), LANES)]

    def store_tile(lanes, value):
        final[:, lanes] = value

    row_norm(
        load_tile, store_tile, tiles, width, mod_ref, 3, total,
        (copies * rows, LANES),
    )
    speed = jnp.dot(
        final[...].astype(jnp.bfloat16), w_mel_ref[...], preferred_element_type=jnp.float32
    )
    first, second = speed[:rows], speed[rows : 2 * rows]
    guided = first + real_ref[0] * (first - second)
    frame = info_ref[1] + lax.broadcasted_iota(jnp.int32, guided.shape, 0)
    velocity = jnp.where(frame < info_ref[0], guided, 0.0)
    velocity_ref[...] = velocity
    estimate_ref[...] = latent_ref[...] + real_ref[1] * velocity


def to_groups(values, subs):
    copies, rows, _ = values.shape
    grouped = values.reshape(copies, subs, rows // subs, HEADS, HEAD_DIM).transpose(0, 3, 1, 2, 4)
    return grouped.reshape(copies * HEADS * subs, rows // subs, HEAD_DIM)


def from_groups(grouped, copies, rows, subs):
    split = grouped.reshape(copies, HEADS, subs, rows // subs, HEAD_DIM).transpose(0, 2, 3, 1, 4)
    return split.reshape(copies, rows, HEADS * HEAD_DIM)


def exchange(values):
    return lax.all_to_all(values, "seq", split_axis=0, concat_axis=1, tiled=True)


def attend_blocks(queries, keys, values, live):
    groups, total, _ = queries.shape
    block = max(size for size in range(1, min(total, 1024) + 1) if total % size == 0)
    blocks = queries.reshape(groups, total // block, block, HEAD_DIM).transpose(1, 0, 2, 3)
    live = live[None, None, :]

    def one_block(query):
        scores = jnp.einsum("gqd,gkd->gqk", query, keys, preferred_element_type=jnp.float32)
        scores = jnp.where(live, scores, NEGATIVE)
        weights = jnp.exp(scores - jnp.max(scores, axis=-1, keepdims=True))
        weights = jnp.where(live, weights, 0.0)
        mixed = jnp.einsum(
            "gqk,gkd->gqd",
            weights.astype(jnp.bfloat16),
            values,
            preferred_element_type=jnp.float32,
        )
        return (mixed / jnp.sum(weights, axis=-1)[..., None]).astype(jnp.bfloat16)

    return lax.map(one_block, blocks).transpose(1, 0, 2, 3).reshape(groups, total, HEAD_DIM)


def attend_any(sent, copies, length):
    groups, _, rows, _ = sent.shape
    count = lax.axis_size("seq")
    pairs = copies * HEADS
    subs = max(1, count // pairs)
    sub_index = lax.axis_index("seq") % subs
    part_rows = rows // subs

    def frames_first(part):
        split = sent[:, part].reshape(copies, groups // copies, rows, LANES)
        return split.transpose(0, 2, 1, 3).reshape(copies, rows, HEADS * HEAD_DIM)

    queries, keys, values = (exchange(to_groups(frames_first(part), subs)) for part in range(3))

    def frames_of(sub):
        start = jnp.arange(count, dtype=jnp.int32)[:, None] * rows + sub * part_rows
        return (start + jnp.arange(part_rows, dtype=jnp.int32)[None, :]).reshape(-1)

    frames = [frames_of(sub_index)]
    parts = [(keys, values)]
    for apart in range(1, subs):
        perm = [(i, i - i % subs + (i + apart) % subs) for i in range(count)]
        parts.append(tuple(lax.ppermute(part, "seq", perm) for part in (keys, values)))
        frames.append(frames_of((sub_index - apart) % subs))
    keys = jnp.concatenate([part[0] for part in parts], axis=1)
    values = jnp.concatenate([part[1] for part in parts], axis=1)
    attended = attend_blocks(queries, keys, values, jnp.concatenate(frames) < length)
    back = lax.all_to_all(attended, "seq", split_axis=1, concat_axis=0, tiled=True)
    joined = from_groups(back, copies, rows, subs)
    split = joined.reshape(copies, rows, groups // copies, LANES).transpose(0, 2, 1, 3)
    return split.reshape(groups, rows, LANES)


def attend_pairs(sent, info):
    count, _, rows, _ = sent.shape
    got = lax.all_to_all(sent, "seq", split_axis=0, concat_axis=0, tiled=True)
    attended = pl.pallas_call(
        attend_kernel,
        name="attend",
        out_shape=jax.ShapeDtypeStruct((count, rows, LANES), jnp.bfloat16),
        in_specs=[smem_spec(), vmem_spec()],
        out_specs=vmem_spec(),
        scratch_shapes=[
            VMEM((count * rows, LANES), jnp.bfloat16),
            VMEM((LANES, count * rows), jnp.bfloat16),
            VMEM((4 * (-(-rows // 16) * 16), LANES), jnp.bfloat16),
        ],
    )(info, got)
    return lax.all_to_all(attended, "seq", split_axis=0, concat_axis=0, tiled=True)


def per_device(
    hidden, latent, lengths, step_index, guidance, modulation, conv_kernel, w_qkv, w_out, w_mel
):
    copies, rows, width = hidden.shape
    count = lax.axis_size("seq")
    offset = lax.axis_index("seq") * rows
    positions = offset + jnp.arange(rows, dtype=jnp.int32)
    info = jnp.stack([lengths[0], offset.astype(jnp.int32)])
    halo = 16
    left = lax.ppermute(hidden[:, rows - halo :], "seq", [(i, i + 1) for i in range(count - 1)])
    right = lax.ppermute(hidden[:, :halo], "seq", [(i + 1, i) for i in range(count - 1)])
    cosine, sine = rotary_tables(positions)
    blocks = HEADS * HEAD_DIM // LANES
    residual, sent = pl.pallas_call(
        front_kernel,
        name="front",
        out_shape=(
            jax.ShapeDtypeStruct((copies, rows, width), jnp.float32),
            jax.ShapeDtypeStruct((copies * blocks, 3, rows, LANES), jnp.bfloat16),
        ),
        in_specs=[smem_spec()] + [vmem_spec()] * 7 + [hbm_spec()],
        out_specs=(vmem_spec(), vmem_spec()),
        scratch_shapes=[
            VMEM((copies, rows + 2 * halo, LANES), jnp.float32),
            VMEM((copies * rows, width), jnp.bfloat16),
            VMEM(w_qkv.shape, jnp.bfloat16),
            pltpu.SemaphoreType.DMA((8,)),
        ],
    )(info, hidden, left, right, conv_kernel, modulation, cosine, sine, w_qkv)
    if count == copies * blocks:
        back = attend_pairs(sent, info)
    else:
        back = attend_any(sent, copies, lengths[0])
    progress = step_index[0].astype(jnp.float32) / STEPS
    time_now = 1.0 - jnp.cos(0.5 * jnp.pi * progress)
    real = jnp.stack([guidance[0], 1.0 - time_now])
    return pl.pallas_call(
        back_kernel,
        name="back",
        out_shape=(
            jax.ShapeDtypeStruct(latent.shape, jnp.float32),
            jax.ShapeDtypeStruct(latent.shape, jnp.float32),
        ),
        in_specs=[smem_spec(), smem_spec()] + [vmem_spec()] * 6,
        out_specs=(vmem_spec(), vmem_spec()),
        scratch_shapes=[
            VMEM((copies * rows, HEADS * HEAD_DIM), jnp.bfloat16),
            VMEM((copies * rows, width), jnp.float32),
        ],
    )(info, real, back, residual, modulation, latent, w_out, w_mel)


def solution(mesh):
    return jax.shard_map(
        per_device,
        mesh=mesh,
        in_specs=(
            P(None, ("clip", "seq"), None),
            P(("clip", "seq"), None),
            P("clip"),
            P(),
            P(),
            P(),
            P(),
            P(),
            P(),
            P(),
        ),
        out_specs=(P(("clip", "seq"), None), P(("clip", "seq"), None)),
        check_vma=False,
    )
```

time: 134 us -> 75.5 us (0.56); the launches traced: 132 us -> 75 us
  local copies, waits for them, and re-layouts: 43.5 us -> 3.29 us
  blocking collectives: 0 us -> 27.5 us
  Pallas kernels: 0 us -> 23.9 us
  starting transfers between devices: 25.1 us -> 7.22 us
  matrix products: 17.7 us -> 0 us
  waiting for transfers between devices: 24.8 us -> 8.23 us
  other arithmetic: 17.8 us -> 2.22 us
    all_to_all x0 -> x1, blocking collectives: none -> 27.5 us  [attend_pairs(): got = lax.all_to_all(sent, 'seq', split_axis=0, concat_axis=0, tiled=True)]
    pallas_call x0 -> x3, Pallas kernels: none -> 23.9 us  [the longest x1 10.1 us: per_device(): pl.pallas_call(front_kernel, name='front', out_shape=(jax.ShapeDtypeStruc...]
    all_to_all x4 -> x1, waiting for transfers between devices: 24.8 us -> 6.47 us  [attend_pairs(): lax.all_to_all(attended, 'seq', split_axis=0, concat_axis=0, tiled=True)]
    all_to_all x4 -> x1, starting transfers between devices: 20.8 us -> 3.53 us  [attend_pairs(): lax.all_to_all(attended, 'seq', split_axis=0, concat_axis=0, tiled=True)]
    unnamed x18 -> x9, local copies, waits for them, and re-layouts: 14.9 us -> 2.28 us
    dot_general x4 -> x0, matrix products: 12 us -> none  [the longest x1 7.27 us: per_device(): jnp.dot(normed.reshape(-1, model_width), w_qkv, preferred_element_type=jn...]
    reshape x6 -> x0, local copies, waits for them, and re-layouts: 9.93 us -> none  [the longest x3 5.91 us: to_groups(): grouped.reshape(copies * HEADS * subs, frame_rows // (2 * subs), 2 * HEAD...]
    reduce_sum x3 -> x0, other arithmetic: 8.68 us -> none  [the longest x1 8.24 us: layer_norm(): mean_value = jnp.mean(values, axis=-1, keepdims=True)]
  transfers between devices with their start and end apart: 6 -> 3, of which waited for: 4 -> 2; matrix products, arithmetic and copies ran while one was open for 25% -> 4% of each run, Pallas kernels for 0% -> 0%
where the time goes in v1:
time: 75.5 us; the launch traced here: 75 us
  blocking collectives  27.5 us (36%)
  Pallas kernels  23.9 us (32%)
  waiting for transfers between devices  8.23 us (11%)
  starting transfers between devices  7.22 us (10%)
  local copies, waits for them, and re-layouts  3.29 us (4%)
  between operations  2.74 us (4%)
  other arithmetic  2.22 us (3%)
    all_to_all x1, blocking collectives, attend_pairs(): got = lax.all_to_all(sent, 'seq', split_axis=0, concat_axis=0, tiled=True)  27.5 us
    pallas_call x1, Pallas kernels, per_device(): pl.pallas_call(front_kernel, name='front', out_shape=(jax.ShapeDtypeStruc...  10.1 us
    pallas_call x1, Pallas kernels, attend_pairs(): pl.pallas_call(attend_kernel, name='attend', out_shape=jax.ShapeDtypeStru...  8.71 us
    all_to_all x1, waiting for transfers between devices, attend_pairs(): lax.all_to_all(attended, 'seq', split_axis=0, concat_axis=0, tiled=True)  6.47 us
    pallas_call x1, Pallas kernels, per_device(): pl.pallas_call(back_kernel, name='back', out_shape=(jax.ShapeDtypeStruct(...  5.08 us
    all_to_all x1, starting transfers between devices, attend_pairs(): lax.all_to_all(attended, 'seq', split_axis=0, concat_axis=0, tiled=True)  3.53 us
    ppermute x1, starting transfers between devices, per_device(): lax.ppermute(hidden[:, rows - halo:], 'seq', [(i, i + 1) for i in range(c...  2.4 us
    unnamed x9, local copies, waits for them, and re-layouts  2.28 us
  transfers between devices with their start and end apart: 3, of which 2 were waited for; matrix products, arithmetic and copies ran while one was open for 4% of the time, Pallas kernels for 0%

profile of v1, /device:TPU:0, one launch (start us, length us, event | category | flops | bytes accessed | tf_op | source)
XLA Modules:
  0.0 75.0 jit_solution(11980208543218485414)
XLA Ops:
  0.6 0.0 copy-start.1
  0.6 1.0 %fusion.1 = (bf16[2,16,1536]{2,1,0:T(8,128)(2,1)S(1)}, bf16[2,16,1536]{2,1,0:T(8,128)(2,1)S(1)}) fusion(bf16[2,56,1536]{2,1,0:T(8,128)(2,1)} %hidden_ref.1), kind=kLoop, calls=%fused_computation.9 | loop fusion | bytes 393216 | tf_op jit(solution)/shard_map/slice | solution.py:343
  1.6 2.4 %collective-permute-start = (bf16[2,16,1536]{2,1,0:T(8,128)(2,1)S(1)}, bf16[2,16,1536]{2,1,0:T(8,128)(2,1)S(1)}, u32[]{:S(2)}, u32[]{:S(2)}) collective-permute-start(bf16[2,16,1536]{2,1,0:T(8,128)(2,1)S(1)} %get-tuple-element.7), channel_id=1, source_target_pairs={{0,1},{1,2},{2,3},{3,4},{4,5},{5,6},{6,7},{7,8},{8,9},{9,10},{10,1... | collective-permute-start | bytes 294920 | tf_op jit(solution)/shard_map/ppermute | solution.py:342
  4.1 1.3 %collective-permute-start.1 = (bf16[2,16,1536]{2,1,0:T(8,128)(2,1)S(1)}, bf16[2,16,1536]{2,1,0:T(8,128)(2,1)S(1)}, u32[]{:S(2)}, u32[]{:S(2)}) collective-permute-start(bf16[2,16,1536]{2,1,0:T(8,128)(2,1)S(1)} %get-tuple-element.6), channel_id=1, source_target_pairs={{1,0},{2,1},{3,2},{4,3},{5,4},{6,5},{7,6},{8,7},{9,8},{10,9},{11,1... | collective-permute-start | bytes 294920 | tf_op jit(solution)/shard_map/ppermute | solution.py:343
  6.0 0.2 fusion
  6.2 0.7 pad_maximum_fusion
  7.0 0.6 pad_add_fusion.info_ref
  7.6 0.0 collective-permute-done.left_ref
  7.6 0.0 copy-start.2
  7.6 1.8 %collective-permute-done.1.right_ref = bf16[2,16,1536]{2,1,0:T(8,128)(2,1)S(1)} collective-permute-done((bf16[2,16,1536]{2,1,0:T(8,128)(2,1)S(1)}, bf16[2,16,1536]{2,1,0:T(8,128)(2,1)S(1)}, u32[]{:S(2)}, u32[]{:S(2)}) %collective-permute-start.1) | collective-permute-done | bytes 98336 | tf_op jit(solution)/shard_map/ppermute | solution.py:343
  9.4 0.0 copy-start.3
  9.4 0.0 copy-done.2
  9.4 0.6 copy-done.3
  10.0 10.1 %front.1 = (f32[2,56,1536]{2,1,0:T(8,128)}, bf16[16,3,56,128]{3,2,1,0:T(8,128)(2,1)}) custom-call(s32[2]{0:T(128)} %pad_add_fusion.info_ref, bf16[2,56,1536]{2,1,0:T(8,128)(2,1)} %hidden_ref.1, bf16[2,16,1536]{2,1,0:T(8,128)(2,1)} %copy-done.2, bf16[2,16,1536]{2,1,0:T(8,128)(2,1)} %copy-done.3, f32[31,1536]{1,0:T(8,128)} %taps_ref.1, f32[5,1536]{1,0:T(8,128)} %mod_ref.3, ...), custom_call_target="tpu_custom_call" | custom-call | tf_op jit(solution)/shard_map/front/pallas_call | solution.py:346
  20.1 27.5 %all_to_all.10.got_ref = bf16[16,3,56,128]{3,2,1,0:T(8,128)(2,1)} all-to-all(bf16[16,3,56,128]{3,2,1,0:T(8,128)(2,1)} %get-tuple-element.4), channel_id=1, replica_groups=mesh['clip'=2,'seq'=16] {'seq'}, dimensions={0} | all-to-all | bytes 1376256 | tf_op jit(solution)/shard_map/all_to_all | solution.py:317
  47.5 8.7 %attend.1 = bf16[16,56,128]{2,1,0:T(8,128)(2,1)} custom-call(s32[2]{0:T(128)} %pad_add_fusion.info_ref, bf16[16,3,56,128]{3,2,1,0:T(8,128)(2,1)} %all_to_all.10.got_ref), custom_call_target="tpu_custom_call" | custom-call | tf_op jit(solution)/shard_map/attend/pallas_call | solution.py:318
  56.3 3.5 %all-to-all-start.1 = ((bf16[16,56,128]{2,1,0:T(8,128)(2,1)}), bf16[16,56,128]{2,1,0:T(8,128)(2,1)S(1)}, u32[]{:S(2)}, u32[]{:S(2)}) async-start(bf16[16,56,128]{2,1,0:T(8,128)(2,1)} %attend.1), calls=%async_computation.1 | async-start | bytes 458752 | tf_op jit(solution)/shard_map/all_to_all | solution.py:330
  59.8 0.0 copy-done.1
  59.8 0.9 %copy.12.w_mel_ref = bf16[1536,100]{1,0:T(8,128)(2,1)} copy(bf16[1536,100]{0,1:T(8,128)(2,1)S(1)} %copy-done.1) | data formatting | bytes 614400 | tf_op args[9]
  62.1 0.6 pad_maximum_fusion.2.real_ref
  62.8 6.5 %all-to-all-done.1.got_ref = bf16[16,56,128]{2,1,0:T(8,128)(2,1)S(1)} async-done(((bf16[16,56,128]{2,1,0:T(8,128)(2,1)}), bf16[16,56,128]{2,1,0:T(8,128)(2,1)S(1)}, u32[]{:S(2)}, u32[]{:S(2)}) %all-to-all-start.1) | async-done | bytes 229408 | tf_op jit(solution)/shard_map/all_to_all | solution.py:330
  69.2 0.0 copy-start
  69.2 0.7 copy-done
  69.9 5.1 %back.1 = (f32[56,100]{1,0:T(8,128)}, f32[56,100]{1,0:T(8,128)}) custom-call(s32[2]{0:T(128)} %pad_add_fusion.info_ref, f32[2]{0:T(128)} %pad_maximum_fusion.2.real_ref, bf16[16,56,128]{2,1,0:T(8,128)(2,1)} %copy-done, f32[2,56,1536]{2,1,0:T(8,128)} %get-tuple-element.5.residual_ref, f32[5,1536]{1,0:T(8,128)} %mod_ref.3, f32[56,100]{1,0:T(8,128)} %latent_ref.1, ...), custom_call_target="tpu_custom_call" | custom-call | tf_op jit(solution)/shard_map/back/pallas_call | solution.py:369
  (2 shorter events, 0.0 us)
Async XLA Ops:
  0.6 59.2 %copy-start.1 = (bf16[1536,100]{0,1:T(8,128)(2,1)S(1)}, bf16[1536,100]{0,1:T(8,128)(2,1)}, u32[]{:S(2)}) copy-start(bf16[1536,100]{0,1:T(8,128)(2,1)} %param.19) | copy-start | bytes 921604
  1.6 6.0 %collective-permute-start = (bf16[2,16,1536]{2,1,0:T(8,128)(2,1)S(1)}, bf16[2,16,1536]{2,1,0:T(8,128)(2,1)S(1)}, u32[]{:S(2)}, u32[]{:S(2)}) collective-permute-start(bf16[2,16,1536]{2,1,0:T(8,128)(2,1)S(1)} %get-tuple-element.7), channel_id=1, source_target_pairs={{0,1},{1,2},{2,3},{3,4},{4,5},{5,6},{6,7},{7,8},{8,9},{9,10},{10,1... | collective-permute-start | bytes 294920 | tf_op jit(solution)/shard_map/ppermute | solution.py:342
  4.1 5.3 %collective-permute-start.1 = (bf16[2,16,1536]{2,1,0:T(8,128)(2,1)S(1)}, bf16[2,16,1536]{2,1,0:T(8,128)(2,1)S(1)}, u32[]{:S(2)}, u32[]{:S(2)}) collective-permute-start(bf16[2,16,1536]{2,1,0:T(8,128)(2,1)S(1)} %get-tuple-element.6), channel_id=1, source_target_pairs={{1,0},{2,1},{3,2},{4,3},{5,4},{6,5},{7,6},{8,7},{9,8},{10,9},{11,1... | collective-permute-start | bytes 294920 | tf_op jit(solution)/shard_map/ppermute | solution.py:343
  7.6 1.8 %copy-start.2 = (bf16[2,16,1536]{2,1,0:T(8,128)(2,1)}, bf16[2,16,1536]{2,1,0:T(8,128)(2,1)S(1)}, u32[]{:S(2)}) copy-start(bf16[2,16,1536]{2,1,0:T(8,128)(2,1)S(1)} %collective-permute-done.left_ref) | copy-start | bytes 294916
  9.4 0.6 copy-start.3
  56.3 13.0 %all-to-all-start.1 = ((bf16[16,56,128]{2,1,0:T(8,128)(2,1)}), bf16[16,56,128]{2,1,0:T(8,128)(2,1)S(1)}, u32[]{:S(2)}, u32[]{:S(2)}) async-start(bf16[16,56,128]{2,1,0:T(8,128)(2,1)} %attend.1), calls=%async_computation.1 | async-start | bytes 458752 | tf_op jit(solution)/shard_map/all_to_all | solution.py:330
  69.2 0.7 copy-start
